TPU v7x, 32 devices: a whole 2x2x4 slice. The times are simulated.
32 devices in a mesh: dp: 2 (over y), seq: 8 (over z, x), head: 2 (over core).
Axes of the slice: x: 2, y: 2, z: 4, core: 2. Of those that a mesh axis runs over, the one named last changes fastest.
Arguments:
- tokens: bfloat16 [2, 2, 1024, 2048], P(None, 'dp', 'seq'), may hold values from -6 to 6
- norm_gain: float32 [2048], replicated, may hold values from 0.5 to 1.5
- w_gate_in: bfloat16 [2048, 4096], P(('dp', 'seq'), 'head'), may hold values from -0.125 to 0.125
- w_x_in: bfloat16 [2048, 4096], P(('dp', 'seq'), 'head'), may hold values from -0.125 to 0.125
- w_bc_in: bfloat16 [2048, 256], P(('dp', 'seq')), may hold values from -0.125 to 0.125
- w_dt_in: bfloat16 [2048, 64], P(('dp', 'seq'), 'head'), may hold values from -0.0625 to 0.0625
- conv_x_w: float32 [4, 4096], P(None, 'head'), may hold values from -3 to 3
- conv_x_b: float32 [4096], P('head'), may hold values from -3 to 3
- conv_bc_w: float32 [4, 256], replicated, may hold values from -3 to 3
- conv_bc_b: float32 [256], replicated, may hold values from -3 to 3
- dt_bias: float32 [64], P('head'), may hold values from -7 to -2
- a_log: float32 [64], P('head'), may hold values from 0 to 1.5
- d_skip: float32 [64], P('head'), may hold values from 0.5 to 1.5
- gate_gain: float32 [4096], P('head'), may hold values from 0.5 to 1.5
- w_out: bfloat16 [4096, 2048], P('head', ('dp', 'seq')), may hold values from -0.09375 to 0.09375
- prefix_len: int32 [2, 2], P(None, 'dp'), may hold values from 102 to 1024, as said below
- cotangent: bfloat16 [2, 2, 1024, 2048], P(None, 'dp', 'seq'), may hold values from -6 to 6
Outputs:
- result: bfloat16 [2, 2, 1024, 2048], P(None, 'dp', 'seq')
- grad_tokens: float32 [2, 2, 1024, 2048], P(None, 'dp', 'seq')
- grad_norm_gain: float32 [2048], replicated
- grad_w_gate_in: float32 [2048, 4096], P(('dp', 'seq'), 'head')
- grad_w_x_in: float32 [2048, 4096], P(('dp', 'seq'), 'head')
- grad_w_bc_in: float32 [2048, 256], P(('dp', 'seq'))
- grad_w_dt_in: float32 [2048, 64], P(('dp', 'seq'), 'head')
- grad_conv_x_w: float32 [4, 4096], P(None, 'head')
- grad_conv_x_b: float32 [4096], P('head')
- grad_conv_bc_w: float32 [4, 256], replicated
- grad_conv_bc_b: float32 [256], replicated
- grad_dt_bias: float32 [64], P('head')
- grad_a_log: float32 [64], P('head')
- grad_d_skip: float32 [64], P('head')
- grad_gate_gain: float32 [4096], P('head')
- grad_w_out: float32 [4096, 2048], P('head', ('dp', 'seq'))
Inputs may be any that keep to these rules, and one draw needn't show every extreme that they name: Tokens before a sequence's prefix_len mix both ways; some sequence has exactly 1024 and some exactly 102.
All inputs are finite; a program needn't handle non-finite values.
Results may differ from a plain program's by a relative error of at most 0.012.
Values may be sent and summed in bfloat16 or wider, within the bound.
A program may use at most 256 MiB of HBM per device.

v0:
```python
import jax
import jax.numpy as jnp
from jax import lax
from jax.sharding import PartitionSpec as P

EPSILON = 1e-05
HIGHEST = lax.Precision.HIGHEST
BF16 = jnp.bfloat16
F32 = jnp.float32
CHUNK = 128


def dot_f32(a, b):
    return jnp.dot(a, b, preferred_element_type=F32)


def causal_conv(signal, kernel, bias):
    margin = kernel.shape[0] - 1
    length = signal.shape[1]
    padded = jnp.pad(signal, ((0, 0), (margin, 0), (0, 0)))
    summed = bias + jnp.zeros_like(signal)
    for offset in range(kernel.shape[0]):
        summed = summed + kernel[offset] * padded[:, offset : offset + length]
    return summed


def mixer(
    prefix, inner, bc, dt_raw, conv_x_w, conv_x_b, conv_bc_w, conv_bc_b, dt_bias, a_log, d_skip
):
    seqs, length, width = inner.shape
    heads = dt_raw.shape[-1]
    state = bc.shape[-1] // 2
    chunk = CHUNK
    count = length // chunk
    values = jax.nn.silu(causal_conv(inner, conv_x_w, conv_x_b))
    active = jax.nn.silu(causal_conv(bc, conv_bc_w, conv_bc_b))
    values = values.reshape(seqs, count, chunk, heads, width // heads)
    b_in = active[..., :state].reshape(seqs, count, chunk, state)
    c_out = active[..., state:].reshape(seqs, count, chunk, state)
    dt = jax.nn.softplus(dt_raw + dt_bias).reshape(seqs, count, chunk, heads)
    cum = jnp.cumsum(dt * -jnp.exp(a_log), axis=2)
    end = cum[:, :, -1:, :]
    places = jnp.arange(length, dtype=jnp.int32).reshape(count, chunk)
    inside = (places[None] < prefix[:, None, None])[..., None]
    weighted = values * dt[..., None]
    ends_state = jnp.einsum(
        "skth,skthp,sktn->skhpn", jnp.exp(end - cum), weighted, b_in, precision=HIGHEST
    )
    back_state = jnp.einsum(
        "skth,skthp,sktn->skhpn",
        jnp.where(inside, jnp.exp(cum), 0.0),
        weighted,
        b_in,
        precision=HIGHEST,
    )
    decay = jnp.exp(end[:, :, 0])[..., None, None]
    zero = jnp.zeros_like(ends_state[:, 0])
    state_in, back_in = ([zero], [zero])
    for k in range(count - 1):
        state_in.append(state_in[-1] * decay[:, k] + ends_state[:, k])
        back_in.append(back_in[-1] * decay[:, count - 1 - k] + back_state[:, count - 1 - k])
    state_in = jnp.stack(state_in, axis=1)
    back_in = jnp.stack(back_in[::-1], axis=1)
    scores = jnp.einsum("sktn,skun->sktu", c_out, b_in, precision=HIGHEST)
    spread = cum[:, :, :, None, :] - cum[:, :, None, :, :]
    behind = (places[:, :, None] >= places[:, None, :])[None, ..., None]
    ahead = (
        (places[:, :, None] < places[:, None, :])[None]
        & (places[None, :, None, :] < prefix[:, None, None, None])
    )[..., None]
    masked = jnp.where(behind, jnp.exp(jnp.where(behind, spread, 0.0)), 0.0) + jnp.where(
        ahead, jnp.exp(jnp.where(ahead, -spread, 0.0)), 0.0
    )
    out = jnp.einsum("sktuh,skuhp->skthp", scores[..., None] * masked, weighted, precision=HIGHEST)
    out = out + jnp.exp(cum)[..., None] * jnp.einsum(
        "sktn,skhpn->skthp", c_out, state_in, precision=HIGHEST
    )
    out = out + jnp.exp(end - cum)[..., None] * jnp.einsum(
        "sktn,skhpn->skthp", c_out, back_in, precision=HIGHEST
    )
    out = out + d_skip[:, None] * values
    return out.reshape(seqs, length, width)


def body(
    tokens,
    norm_gain,
    w_gate_in,
    w_x_in,
    w_bc_in,
    w_dt_in,
    conv_x_w,
    conv_x_b,
    conv_bc_w,
    conv_bc_b,
    dt_bias,
    a_log,
    d_skip,
    gate_gain,
    w_out,
    prefix_len,
    cotangent,
):
    dp, sq, hd = (lax.axis_size("dp"), lax.axis_size("seq"), lax.axis_size("head"))
    me_seq, me_head = (lax.axis_index("seq"), lax.axis_index("head"))
    micro, seqs, span, model = tokens.shape
    group = micro * seqs
    length = span * sq
    rows_here = group * span
    own_rows = rows_here // hd
    half = w_x_in.shape[1]
    width = half // sq
    heads = w_dt_in.shape[1] // sq
    full_inner = half * hd
    prefix = prefix_len.reshape(group)
    everyone = ("seq", "head")

    def mine(x):
        return lax.dynamic_slice_in_dim(
            x.reshape(rows_here, model), me_head * own_rows, own_rows, 0
        )

    def to_sequences(x):
        return x.reshape(sq, group, span, -1).transpose(1, 0, 2, 3).reshape(group, length, -1)

    def from_sequences(x):
        return x.reshape(group, sq, span, -1).transpose(1, 0, 2, 3).reshape(sq * rows_here, -1)

    def rms(x, gain):
        return x * lax.rsqrt(jnp.mean(x * x, axis=-1, keepdims=True) + EPSILON) * gain

    my_tokens = mine(tokens).astype(F32)
    my_cot = mine(cotangent)
    normed_own = rms(my_tokens, norm_gain).astype(BF16)
    normed = lax.all_gather(normed_own, everyone, axis=0, tiled=True)

    def columns(w):
        return lax.all_gather(
            lax.all_to_all(w, "seq", split_axis=1, concat_axis=0, tiled=True),
            "dp",
            axis=0,
            tiled=True,
        )

    wg = columns(w_gate_in)
    wx = columns(w_x_in)
    wd = lax.dynamic_slice_in_dim(
        lax.all_gather(w_dt_in, ("dp", "seq"), axis=0, tiled=True), me_seq * heads, heads, 1
    )
    wb = lax.all_gather(w_bc_in, ("dp", "seq"), axis=0, tiled=True)
    wo = lax.all_gather(
        lax.all_to_all(w_out, "seq", split_axis=0, concat_axis=1, tiled=True),
        "dp",
        axis=1,
        tiled=True,
    )
    cot = lax.all_gather(my_cot, everyone, axis=0, tiled=True)

    def part(x, size, axis):
        return lax.dynamic_slice_in_dim(x, me_seq * size, size, axis)

    cxw, cxb = (part(conv_x_w, width, 1), part(conv_x_b, width, 0))
    dtb, alog, dsk = (part(dt_bias, heads, 0), part(a_log, heads, 0), part(d_skip, heads, 0))
    gain = part(gate_gain, width, 0)

    def project(w):
        return to_sequences(dot_f32(normed, w).astype(BF16)).astype(F32)

    gate, inner, bc, dt_raw = (project(wg), project(wx), project(wb), project(wd))
    mixed, pull = jax.vjp(
        lambda *a: mixer(prefix, *a),
        inner,
        bc,
        dt_raw,
        cxw,
        cxb,
        conv_bc_w,
        conv_bc_b,
        dtb,
        alog,
        dsk,
    )
    sig = jax.nn.sigmoid(gate)
    act = gate * sig
    gated = mixed * act
    grad_scaled = to_sequences(jnp.einsum("rd,kd->rk", cot, wo, preferred_element_type=F32))
    gs = grad_scaled * gain
    sums = lax.psum(
        jnp.stack([jnp.sum(gated * gated, axis=-1), jnp.sum(gs * gated, axis=-1)]), everyone
    )
    scale = lax.rsqrt(sums[0][..., None] / full_inner + EPSILON)
    unit = gated * scale
    scaled = from_sequences((unit * gain).astype(BF16))
    branch = lax.psum_scatter(
        dot_f32(scaled, wo).astype(BF16), everyone, scatter_dimension=0, tiled=True
    )
    result_own = (my_tokens + branch.astype(F32)).astype(BF16)
    grad_gain = jnp.sum(grad_scaled * unit, axis=(0, 1))
    grad_wo = jnp.einsum("rk,rd->kd", scaled, cot, preferred_element_type=F32)
    grad_gated = gs * scale - gated * (scale * scale * scale * (sums[1][..., None] / full_inner))
    grad_mixed = grad_gated * act
    grad_gate = grad_gated * mixed * (sig * (1.0 + gate * (1.0 - sig)))
    d_inner, d_bc, d_dt, d_cxw, d_cxb, d_cbw, d_cbb, d_dtb, d_alog, d_dsk = pull(grad_mixed)
    gg = from_sequences(grad_gate.astype(BF16))
    gx = from_sequences(d_inner.astype(BF16))
    gd = from_sequences(d_dt.astype(BF16))
    gb_own = lax.psum_scatter(
        from_sequences(d_bc), everyone, scatter_dimension=0, tiled=True
    ).astype(BF16)

    def inward(g, w):
        return jnp.einsum("rc,kc->rk", g, w, preferred_element_type=F32)

    def weight_grad(n, g):
        return jnp.einsum("rk,rc->kc", n, g, preferred_element_type=F32)

    part_normed = inward(gg, wg) + inward(gx, wx) + inward(gd, wd)
    grad_normed = lax.psum_scatter(
        part_normed.astype(BF16), everyone, scatter_dimension=0, tiled=True
    ).astype(F32) + inward(gb_own, wb)
    _, pull_norm = jax.vjp(rms, my_tokens, norm_gain)
    grad_rows, grad_norm = pull_norm(grad_normed)
    grad_own = my_cot.astype(F32) + grad_rows

    def home(g):
        return lax.all_to_all(
            lax.psum_scatter(g.astype(BF16), "dp", scatter_dimension=0, tiled=True),
            "seq",
            split_axis=0,
            concat_axis=1,
            tiled=True,
        ).astype(F32)

    g_gate, g_x = (home(weight_grad(normed, gg)), home(weight_grad(normed, gx)))
    g_dt = lax.all_to_all(
        lax.psum_scatter(weight_grad(normed, gd), "dp", scatter_dimension=0, tiled=True),
        "seq",
        split_axis=0,
        concat_axis=1,
        tiled=True,
    )
    g_bc = lax.psum_scatter(
        lax.psum(weight_grad(normed_own, gb_own), "head"),
        ("dp", "seq"),
        scatter_dimension=0,
        tiled=True,
    )
    g_out = lax.all_to_all(
        lax.psum_scatter(grad_wo.astype(BF16), "dp", scatter_dimension=1, tiled=True),
        "seq",
        split_axis=1,
        concat_axis=0,
        tiled=True,
    ).astype(F32)

    def whole(x):
        return lax.all_gather(x, "head", axis=0, tiled=True).reshape(micro, seqs, span, model)

    small = lax.psum((d_cxw, d_cxb, d_dtb, d_alog, d_dsk, grad_gain), "dp")
    small = [lax.all_gather(a, "seq", axis=a.ndim - 1, tiled=True) for a in small]
    grad_norm, d_cbw, d_cbb = lax.psum((grad_norm, d_cbw, d_cbb), ("dp", "seq", "head"))
    return (
        whole(result_own),
        whole(grad_own),
        grad_norm,
        g_gate,
        g_x,
        g_bc,
        g_dt,
        small[0],
        small[1],
        d_cbw,
        d_cbb,
        small[2],
        small[3],
        small[4],
        small[5],
        g_out,
    )


def solution(mesh):
    rows = P(("dp", "seq"), "head")
    tok = P(None, "dp", "seq", None)
    return jax.shard_map(
        body,
        mesh=mesh,
        in_specs=(
            tok,
            P(),
            rows,
            rows,
            P(("dp", "seq"), None),
            rows,
            P(None, "head"),
            P("head"),
            P(),
            P(),
            P("head"),
            P("head"),
            P("head"),
            P("head"),
            P("head", ("dp", "seq")),
            P(None, "dp"),
            tok,
        ),
        out_specs=(
            tok,
            tok,
            P(),
            rows,
            rows,
            P(("dp", "seq"), None),
            rows,
            P(None, "head"),
            P("head"),
            P(),
            P(),
            P("head"),
            P("head"),
            P("head"),
            P("head"),
            P("head", ("dp", "seq")),
        ),
        check_vma=False,
    )
```

profile of v0, /device:TPU:14, one launch (start us, length us, event | category | flops | bytes accessed | tf_op | source)
XLA Modules:
  0.0 1105.0 jit_solution(2029383470495228353)
XLA Ops:
  12.0 27.5 %all_to_all.115 = bf16[128,8,256]{0,2,1:T(8,128)(2,1)S(1)} all-to-all(bf16[128,8,256]{0,2,1:T(8,128)(2,1)S(1)} %bitcast.572), channel_id=1, replica_groups=mesh['dp'=2,'seq'=8,'head'=2] {'seq'}, dimensions={1} | all-to-all | bytes 1048576 | tf_op jit(solution)/shard_map/all_to_all | solution.py:139
  41.4 28.8 %all_to_all.116 = bf16[8,256,128]{2,1,0:T(8,128)(2,1)S(1)} all-to-all(bf16[8,256,128]{2,1,0:T(8,128)(2,1)S(1)} %bitcast.582), channel_id=1, replica_groups=mesh['dp'=2,'seq'=8,'head'=2] {'seq'}, dimensions={0} | all-to-all | bytes 1048576 | tf_op jit(solution)/shard_map/all_to_all | solution.py:152
  83.4 42.2 %all_gather.47 = bf16[2048,32]{0,1:T(8,128)(2,1)S(1)} all-gather(bf16[128,32]{0,1:T(8,128)(2,1)S(1)} %copy-done.97), channel_id=1, replica_groups=mesh['dp'=2,'seq'=8,'head'=2] {'dp','seq'}, dimensions={0}, use_global_device_ids=true | all-gather | bytes 139264 | tf_op jit(solution)/shard_map/all_gather | solution.py:148
  135.8 47.9 %fusion.184 = f32[2,8,128,4]{3,1,2,0:T(8,128)S(1)} fusion(f32[2,8,128,4]{3,1,2,0:T(8,128)S(1)} %copy.524), kind=kOutput, calls=%fused_computation.362 | output fusion | flops 1040384 | bytes 65536 | tf_op jit(solution)/shard_map/jvp(jit(cumsum))/reduce_window_sum | solution.py:41
  198.6 12.3 %all-gather.21.cloned.1.call-done = bf16[256,2048]{0,1:T(8,128)(2,1)} async-done(((bf16[256,1024]{0,1:T(8,128)(2,1)}), bf16[256,2048]{0,1:T(8,128)(2,1)}) %all-gather.21.cloned.1.call-update) | async-done | bytes 1048592 | tf_op jit(solution)/shard_map/all_gather | solution.py:151
  210.9 76.9 %all-gather.19.cloned.1.call-done = bf16[2048,2048]{1,0:T(8,128)(2,1)} async-done(((bf16[128,2048]{1,0:T(8,128)(2,1)}), bf16[2048,2048]{1,0:T(8,128)(2,1)}) %all-gather.19.cloned.1.call-update) | async-done | bytes 8388624 | tf_op jit(solution)/shard_map/all_gather | solution.py:157
  298.3 11.7 %all-gather.17.cloned.1.call-done = bf16[2048,256]{1,0:T(8,128)(2,1)} async-done(((bf16[1024,256]{1,0:T(8,128)(2,1)}), bf16[2048,256]{1,0:T(8,128)(2,1)}) %all-gather.17.cloned.1.call-update) | async-done | bytes 1048592 | tf_op jit(solution)/shard_map/all_gather | solution.py:138
  356.7 10.7 multiply_reduce_fusion.16
  373.1 48.8 %psum.77 = f32[2,2,1024]{2,1,0:T(2,128)S(1)} all-reduce(f32[2,2,1024]{2,1,0:T(2,128)S(1)} %pad_maximum_fusion), channel_id=1, replica_groups=mesh['dp'=2,'seq'=8,'head'=2] {'seq','head'}, use_global_device_ids=true, to_apply=%region_4.5 | all-reduce | flops 4096 | bytes 32768 | tf_op jit(solution)/shard_map/psum | solution.py:188
  455.2 12.5 %fusion.12 = (f32[2,8,128,128]{3,2,1,0:T(8,128)}, f32[2,8,128,128,4]{3,2,4,1,0:T(8,128)}) fusion(f32[2,8,128,4]{2,3,1,0:T(4,128)S(1)} %copy-done.72, pred[2,8,128,128]{3,2,1,0:T(8,128)(4,1)S(1)} %copy-done.51, pred[8,128,128]{2,1,0:T(8,128)(4,1)S(1)} %copy-done.56, f32[2,8,128,128]{3,2,1,0:T(8,128)S(1)} %copy-done.41, ...), kind=kOutput, calls=%fused_computation.18 | convolution fusion | flops 824442880 | bytes 10944512 | tf_op jit(solution)/shard_map/transpose(jvp(sktuh,skuhp->skthp))/dot_general | solution.py:74
  491.9 47.3 %fusion.185 = f32[2,8,128,4]{3,1,2,0:T(8,128)S(1)} fusion(f32[2,8,128,4]{3,1,2,0:T(8,128)S(1)} %copy.609), kind=kOutput, calls=%fused_computation.363 | output fusion | flops 1040384 | bytes 65536 | tf_op jit(solution)/shard_map/transpose(jvp(jit(cumsum)))/reduce_window_sum | solution.py:41
  585.9 16.1 %add_convert_fusion = bf16[2048,2048]{1,0:T(8,128)(2,1)} fusion(f32[2048,2048]{1,0:T(8,128)} %fusion.156, f32[2048,2048]{1,0:T(8,128)} %fusion.189, bf16[2048,256]{1,0:T(8,128)(2,1)S(1)} %bitcast.562, bf16[2048,256]{1,0:T(8,128)(2,1)S(1)} %copy-done.36), kind=kOutput, calls=%fused_computation | convolution fusion | flops 2160066560 | bytes 44040192 | tf_op jit(solution)/shard_map/rc,kc->rk/dot_general | solution.py:212
  640.3 105.5 %reduce-scatter.13.cloned.1.call-done = bf16[128,2048]{1,0:T(8,128)(2,1)} async-done(((bf16[2048,2048]{1,0:T(8,128)(2,1)}), bf16[128,2048]{1,0:T(8,128)(2,1)}) %reduce-scatter.13.cloned.1.call-update) | async-done | bytes 524304 | tf_op jit(solution)/shard_map/reduce_scatter | solution.py:218
  747.9 106.9 %reduce-scatter.11.cloned.1.call-done = bf16[128,2048]{1,0:T(8,128)(2,1)} async-done(((bf16[2048,2048]{1,0:T(8,128)(2,1)}), bf16[128,2048]{1,0:T(8,128)(2,1)}) %reduce-scatter.11.cloned.1.call-update) | async-done | bytes 524304 | tf_op jit(solution)/shard_map/reduce_scatter | solution.py:194
  857.4 19.1 %reduce-scatter.25.cloned.1.call-done = f32[1024,4]{1,0:T(8,128)} async-done(((f32[2048,4]{1,0:T(8,128)}), f32[1024,4]{1,0:T(8,128)}) %reduce-scatter.25.cloned.1.call-update) | async-done | bytes 16400
  877.7 10.1 all_to_all.117
  887.8 11.9 %reduce-scatter.17.cloned.1.call-done = bf16[1024,256]{1,0:T(8,128)(2,1)} async-done(((bf16[2048,256]{1,0:T(8,128)(2,1)}), bf16[1024,256]{1,0:T(8,128)(2,1)}) %reduce-scatter.17.cloned.1.call-update) | async-done | bytes 524304 | tf_op jit(solution)/shard_map/reduce_scatter | solution.py:227
  906.3 16.5 %reduce-scatter.19.cloned.1.call-done = bf16[1024,256]{1,0:T(8,128)(2,1)} async-done(((bf16[2048,256]{1,0:T(8,128)(2,1)}), bf16[1024,256]{1,0:T(8,128)(2,1)}) %reduce-scatter.19.cloned.1.call-update) | async-done | bytes 524304 | tf_op jit(solution)/shard_map/reduce_scatter | solution.py:227
  930.3 15.1 %reduce-scatter.21.cloned.1.call-done = bf16[256,1024]{1,0:T(8,128)(2,1)} async-done(((bf16[256,2048]{1,0:T(8,128)(2,1)}), bf16[256,1024]{1,0:T(8,128)(2,1)}) %reduce-scatter.21.cloned.1.call-update) | async-done | bytes 524304 | tf_op jit(solution)/shard_map/reduce_scatter | solution.py:249
  958.5 19.4 %all-gather = f32[8,1,256]{2,1,0:T(1,128)S(1)} all-gather(f32[1,1,256]{2,1,0:T(1,128)S(1)} %bitcast.633), channel_id=1, replica_groups=mesh['dp'=2,'seq'=8,'head'=2] {'seq'}, dimensions={0}, use_global_device_ids=true | all-gather | bytes 9216 | tf_op jit(solution)/shard_map/all_gather | solution.py:260
  977.9 15.5 %all-gather.1 = f32[8,1,256]{2,1,0:T(1,128)S(1)} all-gather(f32[1,1,256]{2,1,0:T(1,128)S(1)} %bitcast.632), channel_id=1, replica_groups=mesh['dp'=2,'seq'=8,'head'=2] {'seq'}, dimensions={0}, use_global_device_ids=true | all-gather | bytes 9216 | tf_op jit(solution)/shard_map/all_gather | solution.py:260
  993.4 27.9 %all_gather.54 = f32[4,2048]{1,0:T(4,128)S(1)} all-gather(f32[4,256]{1,0:T(4,128)S(1)} %get-tuple-element.164), channel_id=1, replica_groups=mesh['dp'=2,'seq'=8,'head'=2] {'seq'}, dimensions={1}, use_global_device_ids=true | all-gather | bytes 36864 | tf_op jit(solution)/shard_map/all_gather | solution.py:260
  1021.9 22.0 %all-reduce.53 = (f32[32]{0:T(128)}, f32[32]{0:T(128)}, f32[32]{0:T(128)}) all-reduce(f32[32]{0:T(128)S(1)} %dynamic-update-slice, f32[32]{0:T(128)S(1)} %dynamic-update-slice.1, f32[32]{0:T(128)S(1)} %dynamic-update-slice.2), channel_id=1, replica_groups=mesh['dp'=2,'seq'=8,'head'=2] {'seq'}, use_global_device_ids=true, to_apply=%add.49 | all-reduce | flops 96 | bytes 768
  1047.4 43.9 %all-reduce.52 = (f32[2048]{0:T(1024)}, f32[4,256]{1,0:T(4,128)}, f32[256]{0:T(256)}) all-reduce(f32[2048]{0:T(1024)S(1)} %get-tuple-element.135, f32[4,256]{1,0:T(4,128)S(1)} %pad_add_fusion.10, f32[256]{0:T(256)S(1)} %get-tuple-element.131), channel_id=1, replica_groups=mesh['dp'=2,'seq'=8,'head'=2] {'dp','seq','head'}, use_global_device_ids=true, to_apply=%region_33.34 | all-reduce | flops 3328 | bytes 26624 | tf_op jit(solution)/shard_map/psum | solution.py:261
  (445 shorter events, 292.0 us)
Async XLA Ops:
  7.2 122.4 %all-gather.11.cloned.1.call-start = ((), (), s32[]{:S(2)}) async-start(), calls=%async_computation.15 | async-start | bytes 8912896 | tf_op jit(solution)/shard_map/all_gather | solution.py:135
  11.7 172.8 %all-gather.13.cloned.1.call-start = ((), (), s32[]{:S(2)}) async-start(), calls=%async_computation.16 | async-start | bytes 1572864 | tf_op jit(solution)/shard_map/all_gather | solution.py:138
  40.6 151.7 %all-gather.15.cloned.1.call-start = ((), (), s32[]{:S(2)}) async-start(), calls=%async_computation.17 | async-start | bytes 1114112 | tf_op jit(solution)/shard_map/all_gather | solution.py:150
  41.3 169.6 %all-gather.21.cloned.1.call-start = ((), (), s32[]{:S(2)}) async-start(), calls=%async_computation.20 | async-start | bytes 1572864 | tf_op jit(solution)/shard_map/all_gather | solution.py:151
  71.3 216.5 %all-gather.19.cloned.1.call-start = ((), (), s32[]{:S(2)}) async-start(), calls=%async_computation.19 | async-start | bytes 8912896 | tf_op jit(solution)/shard_map/all_gather | solution.py:157
  73.2 55.2 %all-to-all-start.1 = ((bf16[128,8,256]{0,2,1:T(8,128)(2,1)}), bf16[128,8,256]{0,2,1:T(8,128)(2,1)S(1)}, u32[]{:S(2)}, u32[]{:S(2)}) async-start(bf16[128,8,256]{0,2,1:T(8,128)(2,1)} %bitcast.42), calls=%async_computation.1 | async-start | bytes 1048576 | tf_op jit(solution)/shard_map/all_to_all | solution.py:139
  81.6 228.4 %all-gather.17.cloned.1.call-start = ((), (), s32[]{:S(2)}) async-start(), calls=%async_computation.18 | async-start | bytes 1572864 | tf_op jit(solution)/shard_map/all_gather | solution.py:138
  82.6 238.7 %copy-start.81 = (f32[1,256]{1,0:T(1,128)}, f32[1,256]{1,0:T(1,128)S(1)}, u32[]{:S(2)}) copy-start(f32[1,256]{1,0:T(1,128)S(1)} %get-tuple-element.230) | copy-start | bytes 3076
  82.6 238.7 %copy-start.83 = (f32[1,256]{1,0:T(1,128)}, f32[1,256]{1,0:T(1,128)S(1)}, u32[]{:S(2)}) copy-start(f32[1,256]{1,0:T(1,128)S(1)} %get-tuple-element.231) | copy-start | bytes 3076
  82.6 238.7 %copy-start.85 = (f32[1,256]{1,0:T(1,128)}, f32[1,256]{1,0:T(1,128)S(1)}, u32[]{:S(2)}) copy-start(f32[1,256]{1,0:T(1,128)S(1)} %get-tuple-element.232) | copy-start | bytes 3076
  129.5 508.0 %reduce-scatter.15.cloned.1.call-start = ((), (), s32[]{:S(2)}) async-start(), calls=%async_computation.24 | async-start | bytes 2228224 | tf_op jit(solution)/shard_map/reduce_scatter | solution.py:207
  566.1 179.7 %reduce-scatter.13.cloned.1.call-start = ((), (), s32[]{:S(2)}) async-start(), calls=%async_computation.23 | async-start | bytes 8912896 | tf_op jit(solution)/shard_map/reduce_scatter | solution.py:218
  602.0 252.8 %reduce-scatter.11.cloned.1.call-start = ((), (), s32[]{:S(2)}) async-start(), calls=%async_computation.21 | async-start | bytes 8912896 | tf_op jit(solution)/shard_map/reduce_scatter | solution.py:194
  609.1 267.4 %reduce-scatter.25.cloned.1.call-start = ((), (), s32[]{:S(2)}) async-start(), calls=%async_computation.31 | async-start | bytes 1572864
  616.1 283.6 %reduce-scatter.17.cloned.1.call-start = ((), (), s32[]{:S(2)}) async-start(), calls=%async_computation.26 | async-start | bytes 1572864 | tf_op jit(solution)/shard_map/reduce_scatter | solution.py:227
  623.3 299.5 %reduce-scatter.19.cloned.1.call-start = ((), (), s32[]{:S(2)}) async-start(), calls=%async_computation.27 | async-start | bytes 1572864 | tf_op jit(solution)/shard_map/reduce_scatter | solution.py:227
  630.4 315.0 %reduce-scatter.21.cloned.1.call-start = ((), (), s32[]{:S(2)}) async-start(), calls=%async_computation.28 | async-start | bytes 1572864 | tf_op jit(solution)/shard_map/reduce_scatter | solution.py:249
  637.4 406.7 %reduce-scatter.23.cloned.1.call-start = ((), (), s32[]{:S(2)}) async-start(), calls=%async_computation.29 | async-start | bytes 2228224 | tf_op jit(solution)/shard_map/reduce_scatter | solution.py:242
  640.3 451.1 %all-gather.23.cloned.1.call-start = ((), (), s32[]{:S(2)}) async-start(), calls=%async_computation.22 | async-start | bytes 1572864 | tf_op jit(solution)/shard_map/all_gather | solution.py:257
  899.7 23.1 %all-to-all-start.3 = ((bf16[8,128,256]{2,1,0:T(8,128)(2,1)}), bf16[8,128,256]{2,1,0:T(8,128)(2,1)S(1)}, u32[]{:S(2)}, u32[]{:S(2)}) async-start(bf16[8,128,256]{2,1,0:T(8,128)(2,1)} %bitcast.584), calls=%async_computation.7 | async-start | bytes 1048576 | tf_op jit(solution)/shard_map/all_to_all | solution.py:226
  905.7 185.6 %all-gather.25.cloned.1.call-start = ((), (), s32[]{:S(2)}) async-start(), calls=%async_computation.25 | async-start | bytes 3145728 | tf_op jit(solution)/shard_map/all_gather | solution.py:257
  922.8 24.5 %all-to-all-start.4 = ((bf16[8,128,256]{2,1,0:T(8,128)(2,1)}), bf16[8,128,256]{2,1,0:T(8,128)(2,1)S(1)}, u32[]{:S(2)}, u32[]{:S(2)}) async-start(bf16[8,128,256]{2,1,0:T(8,128)(2,1)} %bitcast.583), calls=%async_computation.9 | async-start | bytes 1048576 | tf_op jit(solution)/shard_map/all_to_all | solution.py:226
  947.3 99.0 %all-to-all-start.6 = ((bf16[256,8,128]{2,0,1:T(8,128)(2,1)}), bf16[256,8,128]{2,0,1:T(8,128)(2,1)S(1)}, u32[]{:S(2)}, u32[]{:S(2)}) async-start(bf16[256,8,128]{2,0,1:T(8,128)(2,1)} %copy_bitcast_fusion), calls=%async_computation.12 | async-start | bytes 1048576 | tf_op jit(solution)/shard_map/all_to_all | solution.py:248
  953.4 138.0 %all-reduce.57.cloned.1.call-start = ((), (), s32[]{:S(2)}) async-start(), calls=%async_computation.30 | async-start | bytes 262144 | tf_op jit(solution)/shard_map/psum | solution.py:243
  (114 other events, 4277.4 us)
Sparse Core Ops, SparseCore 0:
  11.8 92.2 all-gather.10
  106.2 24.0 all-gather.12
  133.1 54.8 all-gather.14
  190.0 20.8 all-gather.20
  213.5 74.2 all-gather.18
  289.8 20.1 all-gather.16
  566.2 70.9 reduce-scatter.14
  641.8 103.9 reduce-scatter.12
  750.4 104.3 reduce-scatter.10
  857.6 18.9 reduce-scatter.24
  879.3 20.3 reduce-scatter.16
  902.5 20.3 reduce-scatter.18
  925.1 20.3 reduce-scatter.20
  948.2 76.7 reduce-scatter.22
  1026.4 14.1 all-gather.22
  1042.7 11.7 all-gather.24
  1056.8 19.0 all-reduce.56
where the time goes:
time: 1110 us; the launch traced here: 1100 us
  waiting for transfers between devices  377 us (34%)
  blocking collectives  291 us (26%)
  matrix products  176 us (16%)
  other arithmetic  145 us (13%)
  local copies, waits for them, and re-layouts  72 us (6%)
  starting transfers between devices  27.2 us (2%)
  between operations  16.4 us (1%)
    reduce_scatter x1, waiting for transfers between devices, body(): lax.psum_scatter(dot_f32(scaled, wo).astype(BF16), everyone, scatter_dime...  107 us
    reduce_scatter x1, waiting for transfers between devices, body(): lax.psum_scatter(part_normed.astype(BF16), everyone, scatter_dimension=0,...  105 us
    another operation x2, other arithmetic, mixer(): cum = jnp.cumsum(dt * -jnp.exp(a_log), axis=2)  95.2 us
    all_gather x1, waiting for transfers between devices, body(): cot = lax.all_gather(my_cot, everyone, axis=0, tiled=True)  76.9 us
    all_gather x3, blocking collectives, body(): lax.all_gather(a, 'seq', axis=a.ndim - 1, tiled=True)  62.8 us
    psum x1, blocking collectives, body(): lax.psum(jnp.stack([jnp.sum(gated * gated, axis=-1), jnp.sum(gs * gated,...  48.8 us
    psum x1, blocking collectives, body(): lax.psum((grad_norm, d_cbw, d_cbb), ('dp', 'seq', 'head'))  43.9 us
    all_gather x1, blocking collectives, body(): lax.all_gather(w_dt_in, ('dp', 'seq'), axis=0, tiled=True)  42.2 us
  transfers between devices with their start and end apart: 21, of which 9 were waited for; matrix products, arithmetic and copies ran while one was open for 16% of the time, Pallas kernels for 0%

commit v1 on v0

--- a/solution.py
+++ b/solution.py
@@ -258,7 +258,7 @@
 
     small = lax.psum((d_cxw, d_cxb, d_dtb, d_alog, d_dsk, grad_gain), "dp")
     small = [lax.all_gather(a, "seq", axis=a.ndim - 1, tiled=True) for a in small]
-    grad_norm, d_cbw, d_cbb = lax.psum((grad_norm, d_cbw, d_cbb), ("dp", "seq", "head"))
+    grad_norm, d_cbw, d_cbb = lax.psum(lax.psum((grad_norm, d_cbw, d_cbb), ("seq", "head")), "dp")
     return (
         whole(result_own),
         whole(grad_own),

time: 1110 us -> 1210 us (1.090)
  waiting for transfers between devices: 377 us -> 449 us
  blocking collectives: 291 us -> 311 us
    reduce_scatter x1, waiting for transfers between devices: 0.02 us -> 71.1 us  [body(): lax.psum_scatter(lax.psum(weight_grad(normed_own, gb_own), 'head'), ('dp'...]
  transfers between devices with their start and end apart: 21 -> 21, of which waited for: 9 -> 10; matrix products, arithmetic and copies ran while one was open for 16% -> 14% of each run, Pallas kernels for 0% -> 0%
where the time goes in v1:
time: 1210 us; the launch traced here: 1200 us
  waiting for transfers between devices  449 us (37%)
  blocking collectives  311 us (26%)
  matrix products  176 us (15%)
  other arithmetic  145 us (12%)
  local copies, waits for them, and re-layouts  72 us (6%)
  starting transfers between devices  27.2 us (2%)
  between operations  16.4 us (1%)
    reduce_scatter x1, waiting for transfers between devices, body(): lax.psum_scatter(dot_f32(scaled, wo).astype(BF16), everyone, scatter_dime...  107 us
    reduce_scatter x1, waiting for transfers between devices, body(): lax.psum_scatter(part_normed.astype(BF16), everyone, scatter_dimension=0,...  106 us
    another operation x2, other arithmetic, mixer(): cum = jnp.cumsum(dt * -jnp.exp(a_log), axis=2)  95.2 us
    all_gather x1, waiting for transfers between devices, body(): cot = lax.all_gather(my_cot, everyone, axis=0, tiled=True)  76.9 us
    reduce_scatter x1, waiting for transfers between devices, body(): lax.psum_scatter(lax.psum(weight_grad(normed_own, gb_own), 'head'), ('dp'...  71.1 us
    all_gather x3, blocking collectives, body(): lax.all_gather(a, 'seq', axis=a.ndim - 1, tiled=True)  70.4 us
    psum x1, blocking collectives, body(): lax.psum((grad_norm, d_cbw, d_cbb), ('seq', 'head'))  53.1 us
    psum x1, blocking collectives, body(): lax.psum(jnp.stack([jnp.sum(gated * gated, axis=-1), jnp.sum(gs * gated,...  48.8 us
  transfers between devices with their start and end apart: 21, of which 10 were waited for; matrix products, arithmetic and copies ran while one was open for 14% of the time, Pallas kernels for 0%

profile of v1, /device:TPU:14, one launch (start us, length us, event | category | flops | bytes accessed | tf_op | source)
XLA Modules:
  0.0 1196.3 jit_solution(2877715779639987504)
XLA Ops:
  12.0 27.5 %all_to_all.115 = bf16[128,8,256]{0,2,1:T(8,128)(2,1)S(1)} all-to-all(bf16[128,8,256]{0,2,1:T(8,128)(2,1)S(1)} %bitcast.572), channel_id=1, replica_groups=mesh['dp'=2,'seq'=8,'head'=2] {'seq'}, dimensions={1} | all-to-all | bytes 1048576 | tf_op jit(solution)/shard_map/all_to_all | solution.py:139
  41.4 28.8 %all_to_all.116 = bf16[8,256,128]{2,1,0:T(8,128)(2,1)S(1)} all-to-all(bf16[8,256,128]{2,1,0:T(8,128)(2,1)S(1)} %bitcast.582), channel_id=1, replica_groups=mesh['dp'=2,'seq'=8,'head'=2] {'seq'}, dimensions={0} | all-to-all | bytes 1048576 | tf_op jit(solution)/shard_map/all_to_all | solution.py:152
  83.4 42.2 %all_gather.47 = bf16[2048,32]{0,1:T(8,128)(2,1)S(1)} all-gather(bf16[128,32]{0,1:T(8,128)(2,1)S(1)} %copy-done.97), channel_id=1, replica_groups=mesh['dp'=2,'seq'=8,'head'=2] {'dp','seq'}, dimensions={0}, use_global_device_ids=true | all-gather | bytes 139264 | tf_op jit(solution)/shard_map/all_gather | solution.py:148
  135.8 47.9 %fusion.184 = f32[2,8,128,4]{3,1,2,0:T(8,128)S(1)} fusion(f32[2,8,128,4]{3,1,2,0:T(8,128)S(1)} %copy.524), kind=kOutput, calls=%fused_computation.362 | output fusion | flops 1040384 | bytes 65536 | tf_op jit(solution)/shard_map/jvp(jit(cumsum))/reduce_window_sum | solution.py:41
  198.6 12.3 %all-gather.21.cloned.1.call-done = bf16[256,2048]{0,1:T(8,128)(2,1)} async-done(((bf16[256,1024]{0,1:T(8,128)(2,1)}), bf16[256,2048]{0,1:T(8,128)(2,1)}) %all-gather.21.cloned.1.call-update) | async-done | bytes 1048592 | tf_op jit(solution)/shard_map/all_gather | solution.py:151
  210.9 76.9 %all-gather.19.cloned.1.call-done = bf16[2048,2048]{1,0:T(8,128)(2,1)} async-done(((bf16[128,2048]{1,0:T(8,128)(2,1)}), bf16[2048,2048]{1,0:T(8,128)(2,1)}) %all-gather.19.cloned.1.call-update) | async-done | bytes 8388624 | tf_op jit(solution)/shard_map/all_gather | solution.py:157
  298.3 11.7 all-gather.17.cloned.1.call-done
  356.7 10.7 multiply_reduce_fusion.16
  373.1 48.8 %psum.98 = f32[2,2,1024]{2,1,0:T(2,128)S(1)} all-reduce(f32[2,2,1024]{2,1,0:T(2,128)S(1)} %pad_maximum_fusion), channel_id=1, replica_groups=mesh['dp'=2,'seq'=8,'head'=2] {'seq','head'}, use_global_device_ids=true, to_apply=%region_4.5 | all-reduce | flops 4096 | bytes 32768 | tf_op jit(solution)/shard_map/psum | solution.py:188
  455.2 12.5 %fusion.12 = (f32[2,8,128,128]{3,2,1,0:T(8,128)}, f32[2,8,128,128,4]{3,2,4,1,0:T(8,128)}) fusion(f32[2,8,128,4]{2,3,1,0:T(4,128)S(1)} %copy-done.72, pred[2,8,128,128]{3,2,1,0:T(8,128)(4,1)S(1)} %copy-done.51, pred[8,128,128]{2,1,0:T(8,128)(4,1)S(1)} %copy-done.56, f32[2,8,128,128]{3,2,1,0:T(8,128)S(1)} %copy-done.41, ...), kind=kOutput, calls=%fused_computation.18 | convolution fusion | flops 824442880 | bytes 10944512 | tf_op jit(solution)/shard_map/transpose(jvp(sktuh,skuhp->skthp))/dot_general | solution.py:74
  491.9 47.3 %fusion.185 = f32[2,8,128,4]{3,1,2,0:T(8,128)S(1)} fusion(f32[2,8,128,4]{3,1,2,0:T(8,128)S(1)} %copy.609), kind=kOutput, calls=%fused_computation.363 | output fusion | flops 1040384 | bytes 65536 | tf_op jit(solution)/shard_map/transpose(jvp(jit(cumsum)))/reduce_window_sum | solution.py:41
  585.9 16.1 %add_convert_fusion = bf16[2048,2048]{1,0:T(8,128)(2,1)} fusion(f32[2048,2048]{1,0:T(8,128)} %fusion.156, f32[2048,2048]{1,0:T(8,128)} %fusion.189, bf16[2048,256]{1,0:T(8,128)(2,1)S(1)} %bitcast.562, bf16[2048,256]{1,0:T(8,128)(2,1)S(1)} %copy-done.36), kind=kOutput, calls=%fused_computation | convolution fusion | flops 2160066560 | bytes 44040192 | tf_op jit(solution)/shard_map/rc,kc->rk/dot_general | solution.py:212
  640.3 105.6 %reduce-scatter.13.cloned.1.call-done = bf16[128,2048]{1,0:T(8,128)(2,1)} async-done(((bf16[2048,2048]{1,0:T(8,128)(2,1)}), bf16[128,2048]{1,0:T(8,128)(2,1)}) %reduce-scatter.13.cloned.1.call-update) | async-done | bytes 524304 | tf_op jit(solution)/shard_map/reduce_scatter | solution.py:218
  748.0 107.0 %reduce-scatter.11.cloned.1.call-done = bf16[128,2048]{1,0:T(8,128)(2,1)} async-done(((bf16[2048,2048]{1,0:T(8,128)(2,1)}), bf16[128,2048]{1,0:T(8,128)(2,1)}) %reduce-scatter.11.cloned.1.call-update) | async-done | bytes 524304 | tf_op jit(solution)/shard_map/reduce_scatter | solution.py:194
  857.6 19.1 %reduce-scatter.25.cloned.1.call-done = f32[1024,4]{1,0:T(8,128)} async-done(((f32[2048,4]{1,0:T(8,128)}), f32[1024,4]{1,0:T(8,128)}) %reduce-scatter.25.cloned.1.call-update) | async-done | bytes 16400
  888.0 11.8 reduce-scatter.17.cloned.1.call-done
  906.5 16.5 %reduce-scatter.19.cloned.1.call-done = bf16[1024,256]{1,0:T(8,128)(2,1)} async-done(((bf16[2048,256]{1,0:T(8,128)(2,1)}), bf16[1024,256]{1,0:T(8,128)(2,1)}) %reduce-scatter.19.cloned.1.call-update) | async-done | bytes 524304 | tf_op jit(solution)/shard_map/reduce_scatter | solution.py:227
  930.3 15.3 %reduce-scatter.21.cloned.1.call-done = bf16[256,1024]{1,0:T(8,128)(2,1)} async-done(((bf16[256,2048]{1,0:T(8,128)(2,1)}), bf16[256,1024]{1,0:T(8,128)(2,1)}) %reduce-scatter.21.cloned.1.call-update) | async-done | bytes 524304 | tf_op jit(solution)/shard_map/reduce_scatter | solution.py:249
  954.0 71.1 %reduce-scatter.23.cloned.1.call-done = f32[128,256]{1,0:T(8,128)} async-done(((f32[2048,256]{1,0:T(8,128)}), f32[128,256]{1,0:T(8,128)}) %reduce-scatter.23.cloned.1.call-update) | async-done | bytes 131088 | tf_op jit(solution)/shard_map/reduce_scatter | solution.py:242
  1028.4 53.1 %all-reduce.52 = (f32[2048]{0:T(1024)S(1)}, f32[4,256]{1,0:T(4,128)S(1)}, f32[256]{0:T(256)S(1)}) all-reduce(f32[2048]{0:T(1024)S(1)} %get-tuple-element.135, f32[4,256]{1,0:T(4,128)S(1)} %pad_add_fusion.10, f32[256]{0:T(256)S(1)} %get-tuple-element.131), channel_id=1, replica_groups=mesh['dp'=2,'seq'=8,'head'=2] {'seq','head'}, use_global_device_ids=true, to_apply=%region_33.34 | all-reduce | flops 3328 | bytes 26624 | tf_op jit(solution)/shard_map/psum | solution.py:261
  1089.4 26.4 %all-gather = f32[8,1,256]{2,1,0:T(1,128)S(1)} all-gather(f32[1,1,256]{2,1,0:T(1,128)S(1)} %bitcast.633), channel_id=1, replica_groups=mesh['dp'=2,'seq'=8,'head'=2] {'seq'}, dimensions={0}, use_global_device_ids=true | all-gather | bytes 9216 | tf_op jit(solution)/shard_map/all_gather | solution.py:260
  1115.8 16.3 %all-gather.1 = f32[8,1,256]{2,1,0:T(1,128)S(1)} all-gather(f32[1,1,256]{2,1,0:T(1,128)S(1)} %bitcast.632), channel_id=1, replica_groups=mesh['dp'=2,'seq'=8,'head'=2] {'seq'}, dimensions={0}, use_global_device_ids=true | all-gather | bytes 9216 | tf_op jit(solution)/shard_map/all_gather | solution.py:260
  1132.1 27.7 %all_gather.54 = f32[4,2048]{1,0:T(4,128)S(1)} all-gather(f32[4,256]{1,0:T(4,128)S(1)} %get-tuple-element.165), channel_id=1, replica_groups=mesh['dp'=2,'seq'=8,'head'=2] {'seq'}, dimensions={1}, use_global_device_ids=true | all-gather | bytes 36864 | tf_op jit(solution)/shard_map/all_gather | solution.py:260
  1160.4 22.3 %all-reduce.53 = (f32[32]{0:T(128)}, f32[32]{0:T(128)}, f32[32]{0:T(128)}) all-reduce(f32[32]{0:T(128)S(1)} %dynamic-update-slice, f32[32]{0:T(128)S(1)} %dynamic-update-slice.1, f32[32]{0:T(128)S(1)} %dynamic-update-slice.2), channel_id=1, replica_groups=mesh['dp'=2,'seq'=8,'head'=2] {'seq'}, use_global_device_ids=true, to_apply=%add.49 | all-reduce | flops 96 | bytes 768
  (445 shorter events, 304.9 us)
Async XLA Ops:
  7.2 122.4 %all-gather.11.cloned.1.call-start = ((), (), s32[]{:S(2)}) async-start(), calls=%async_computation.15 | async-start | bytes 8912896 | tf_op jit(solution)/shard_map/all_gather | solution.py:135
  11.7 172.8 %all-gather.13.cloned.1.call-start = ((), (), s32[]{:S(2)}) async-start(), calls=%async_computation.16 | async-start | bytes 1572864 | tf_op jit(solution)/shard_map/all_gather | solution.py:138
  40.6 151.7 %all-gather.15.cloned.1.call-start = ((), (), s32[]{:S(2)}) async-start(), calls=%async_computation.17 | async-start | bytes 1114112 | tf_op jit(solution)/shard_map/all_gather | solution.py:150
  41.3 169.6 %all-gather.21.cloned.1.call-start = ((), (), s32[]{:S(2)}) async-start(), calls=%async_computation.20 | async-start | bytes 1572864 | tf_op jit(solution)/shard_map/all_gather | solution.py:151
  71.3 216.5 %all-gather.19.cloned.1.call-start = ((), (), s32[]{:S(2)}) async-start(), calls=%async_computation.19 | async-start | bytes 8912896 | tf_op jit(solution)/shard_map/all_gather | solution.py:157
  73.2 55.2 %all-to-all-start.1 = ((bf16[128,8,256]{0,2,1:T(8,128)(2,1)}), bf16[128,8,256]{0,2,1:T(8,128)(2,1)S(1)}, u32[]{:S(2)}, u32[]{:S(2)}) async-start(bf16[128,8,256]{0,2,1:T(8,128)(2,1)} %bitcast.42), calls=%async_computation.1 | async-start | bytes 1048576 | tf_op jit(solution)/shard_map/all_to_all | solution.py:139
  81.6 228.4 %all-gather.17.cloned.1.call-start = ((), (), s32[]{:S(2)}) async-start(), calls=%async_computation.18 | async-start | bytes 1572864 | tf_op jit(solution)/shard_map/all_gather | solution.py:138
  82.6 238.7 %copy-start.81 = (f32[1,256]{1,0:T(1,128)}, f32[1,256]{1,0:T(1,128)S(1)}, u32[]{:S(2)}) copy-start(f32[1,256]{1,0:T(1,128)S(1)} %get-tuple-element.233) | copy-start | bytes 3076
  82.6 238.7 %copy-start.83 = (f32[1,256]{1,0:T(1,128)}, f32[1,256]{1,0:T(1,128)S(1)}, u32[]{:S(2)}) copy-start(f32[1,256]{1,0:T(1,128)S(1)} %get-tuple-element.234) | copy-start | bytes 3076
  82.6 238.7 %copy-start.85 = (f32[1,256]{1,0:T(1,128)}, f32[1,256]{1,0:T(1,128)S(1)}, u32[]{:S(2)}) copy-start(f32[1,256]{1,0:T(1,128)S(1)} %get-tuple-element.235) | copy-start | bytes 3076
  129.5 508.0 %reduce-scatter.15.cloned.1.call-start = ((), (), s32[]{:S(2)}) async-start(), calls=%async_computation.24 | async-start | bytes 2228224 | tf_op jit(solution)/shard_map/reduce_scatter | solution.py:207
  566.1 179.8 %reduce-scatter.13.cloned.1.call-start = ((), (), s32[]{:S(2)}) async-start(), calls=%async_computation.23 | async-start | bytes 8912896 | tf_op jit(solution)/shard_map/reduce_scatter | solution.py:218
  602.0 253.0 %reduce-scatter.11.cloned.1.call-start = ((), (), s32[]{:S(2)}) async-start(), calls=%async_computation.21 | async-start | bytes 8912896 | tf_op jit(solution)/shard_map/reduce_scatter | solution.py:194
  609.1 267.6 %reduce-scatter.25.cloned.1.call-start = ((), (), s32[]{:S(2)}) async-start(), calls=%async_computation.31 | async-start | bytes 1572864
  616.1 283.8 %reduce-scatter.17.cloned.1.call-start = ((), (), s32[]{:S(2)}) async-start(), calls=%async_computation.26 | async-start | bytes 1572864 | tf_op jit(solution)/shard_map/reduce_scatter | solution.py:227
  623.3 299.7 %reduce-scatter.19.cloned.1.call-start = ((), (), s32[]{:S(2)}) async-start(), calls=%async_computation.27 | async-start | bytes 1572864 | tf_op jit(solution)/shard_map/reduce_scatter | solution.py:227
  630.4 315.2 %reduce-scatter.21.cloned.1.call-start = ((), (), s32[]{:S(2)}) async-start(), calls=%async_computation.28 | async-start | bytes 1572864 | tf_op jit(solution)/shard_map/reduce_scatter | solution.py:249
  637.4 387.7 %reduce-scatter.23.cloned.1.call-start = ((), (), s32[]{:S(2)}) async-start(), calls=%async_computation.29 | async-start | bytes 2228224 | tf_op jit(solution)/shard_map/reduce_scatter | solution.py:242
  640.3 542.4 %all-gather.23.cloned.1.call-start = ((), (), s32[]{:S(2)}) async-start(), calls=%async_computation.22 | async-start | bytes 1572864 | tf_op jit(solution)/shard_map/all_gather | solution.py:257
  899.9 23.1 %all-to-all-start.3 = ((bf16[8,128,256]{2,1,0:T(8,128)(2,1)}), bf16[8,128,256]{2,1,0:T(8,128)(2,1)S(1)}, u32[]{:S(2)}, u32[]{:S(2)}) async-start(bf16[8,128,256]{2,1,0:T(8,128)(2,1)} %bitcast.584), calls=%async_computation.7 | async-start | bytes 1048576 | tf_op jit(solution)/shard_map/all_to_all | solution.py:226
  905.9 276.8 %all-gather.25.cloned.1.call-start = ((), (), s32[]{:S(2)}) async-start(), calls=%async_computation.25 | async-start | bytes 3145728 | tf_op jit(solution)/shard_map/all_gather | solution.py:257
  923.0 24.5 %all-to-all-start.4 = ((bf16[8,128,256]{2,1,0:T(8,128)(2,1)}), bf16[8,128,256]{2,1,0:T(8,128)(2,1)S(1)}, u32[]{:S(2)}, u32[]{:S(2)}) async-start(bf16[8,128,256]{2,1,0:T(8,128)(2,1)} %bitcast.583), calls=%async_computation.9 | async-start | bytes 1048576 | tf_op jit(solution)/shard_map/all_to_all | solution.py:226
  947.5 79.8 %all-to-all-start.6 = ((bf16[256,8,128]{2,0,1:T(8,128)(2,1)}), bf16[256,8,128]{2,0,1:T(8,128)(2,1)S(1)}, u32[]{:S(2)}, u32[]{:S(2)}) async-start(bf16[256,8,128]{2,0,1:T(8,128)(2,1)} %copy_bitcast_fusion), calls=%async_computation.12 | async-start | bytes 1048576 | tf_op jit(solution)/shard_map/all_to_all | solution.py:248
  953.5 229.2 %all-reduce.57.cloned.1.call-start = ((), (), s32[]{:S(2)}) async-start(), calls=%async_computation.30 | async-start | bytes 262144 | tf_op jit(solution)/shard_map/psum | solution.py:243
  (114 other events, 4285.6 us)
Sparse Core Ops, SparseCore 0:
  11.8 92.2 all-gather.10
  106.2 24.0 all-gather.12
  133.1 54.8 all-gather.14
  190.0 20.8 all-gather.20
  213.5 74.2 all-gather.18
  289.8 20.1 all-gather.16
  566.2 70.9 reduce-scatter.14
  641.8 104.0 reduce-scatter.12
  750.5 104.4 reduce-scatter.10
  857.7 18.9 reduce-scatter.24
  879.5 20.2 reduce-scatter.16
  902.6 20.3 reduce-scatter.18
  925.2 20.3 reduce-scatter.20
  948.4 76.6 reduce-scatter.22
  1026.5 14.3 all-gather.22
  1042.9 11.7 all-gather.24
  1057.0 19.0 all-reduce.56
